TPU v7x, 32 devices: a whole 2x2x4 slice. The times are simulated.
32 devices in a mesh: str: 8 (over z, x), fac: 4 (over y, core).
Axes of the slice: x: 2, y: 2, z: 4, core: 2. Of those that a mesh axis runs over, the one named last changes fastest.
Arguments:
- amplitudes: bfloat16 [2, 4096, 4096], P(None, 'str'), may hold values from -6 to 6
- beta_index: int32 [2, 32, 12], replicated, may hold values from 0 to 31, all different within a row; in each aligned block of 32 rows (0 to 31, 32 to 63, ..., all dimensions but the last counted through in order) at most 24 rows name the same one
- beta_tile: int32 [2, 12], replicated, may hold values from 0 to 15
- beta_flip: int32 [2, 4096], replicated, may hold values 0 or 1
- alpha_index: int32 [2, 32, 12], replicated, may hold values from 0 to 31, all different within a row; in each aligned block of 32 rows (0 to 31, 32 to 63, ..., all dimensions but the last counted through in order) at most 24 rows name the same one
- alpha_tile: int32 [2, 12], replicated, may hold values from 0 to 15
- alpha_flip: int32 [2, 4096], replicated, may hold values 0 or 1
- beta_tiles: bfloat16 [16, 128, 128], replicated, may hold values from -0.15625 to 0.15625
- alpha_tiles: bfloat16 [16, 128, 128], replicated, may hold values from -0.109375 to 0.109375
Outputs:
- sigma: float32 [2, 4096, 4096], P(None, 'fac', 'str')
Inputs may be any that keep to these rules, and one draw needn't show every extreme that they name: `beta_index`: each block row of one factor's beta operator names 12 different block columns; within one factor's operator no block column is named by more than 24 block rows, and in some factor one column is named by exactly 24. `alpha_index`: each block row of one factor's alpha operator names 12 different block columns; within one factor's operator no block column is named by more than 24 block rows, and in some factor one column is named by exactly 24.
All inputs are finite; a program needn't handle non-finite values.
Results may differ from a plain program's by a relative error of at most 0.012.
Values may be sent and summed in bfloat16 or wider, within the bound.
A program may use at most 128 MiB of HBM per device.

v0:
```python
import jax
import jax.numpy as jnp
from jax import lax
from jax.sharding import PartitionSpec as P


def apply_beta(amplitudes, block_ids, tile_ids, flips, tile_table):
    part_count, height, column_count = amplitudes.shape
    tile_size = tile_table.shape[1]
    block_count = column_count // tile_size
    signs = (1 - 2 * flips).astype(jnp.bfloat16)
    signed = amplitudes * signs[None, None, :]
    blocks = signed.reshape(part_count, height, block_count, tile_size)
    weights = tile_table[tile_ids]
    group_size = block_count // 4
    pieces = []
    for group_id in range(4):
        lower = group_id * group_size
        chosen = block_ids[lower : lower + group_size]
        gathered = blocks[:, :, chosen]
        pieces.append(
            jnp.einsum(
                "pajkc,krc->pajr", gathered, weights, preferred_element_type=jnp.float32
            ).astype(jnp.bfloat16)
        )
    return jnp.concatenate(pieces, axis=2).reshape(part_count, height, column_count)


def apply_alpha(half, block_ids, tile_ids, flips, tile_table):
    part_count, total, column_count = half.shape
    tile_size = tile_table.shape[1]
    block_count = total // tile_size
    signs = (1 - 2 * flips).astype(jnp.bfloat16)
    signed = half * signs[None, :, None]
    blocks = signed.reshape(part_count, block_count, tile_size, column_count)
    weights = tile_table[tile_ids]
    group_size = block_count // 4
    pieces = []
    for group_id in range(4):
        lower = group_id * group_size
        chosen = block_ids[lower : lower + group_size]
        gathered = blocks[:, chosen]
        pieces.append(
            jnp.einsum(
                "pjkcn,krc->pjrn", gathered, weights, preferred_element_type=jnp.float32
            ).astype(jnp.bfloat16)
        )
    return jnp.concatenate(pieces, axis=1).reshape(part_count, total, column_count)


def local(
    amplitudes,
    beta_index,
    beta_tile,
    beta_flip,
    alpha_index,
    alpha_tile,
    alpha_flip,
    beta_tiles,
    alpha_tiles,
):
    position = lax.axis_index("fac")
    factor = position // 2
    part = position % 2
    own_part = lax.dynamic_index_in_dim(amplitudes, part, 0, keepdims=True)
    beta_ids = lax.dynamic_index_in_dim(beta_index, factor, 0, keepdims=False)
    beta_kinds = lax.dynamic_index_in_dim(beta_tile, factor, 0, keepdims=False)
    beta_signs = lax.dynamic_index_in_dim(beta_flip, factor, 0, keepdims=False)
    half = apply_beta(own_part, beta_ids, beta_kinds, beta_signs, beta_tiles)
    alpha_ids = lax.dynamic_index_in_dim(alpha_index, factor, 0, keepdims=False)
    alpha_kinds = lax.dynamic_index_in_dim(alpha_tile, factor, 0, keepdims=False)
    alpha_signs = lax.dynamic_index_in_dim(alpha_flip, factor, 0, keepdims=False)
    mixed = apply_alpha(
        lax.all_to_all(half, "str", split_axis=2, concat_axis=1, tiled=True),
        alpha_ids,
        alpha_kinds,
        alpha_signs,
        alpha_tiles,
    )
    mixed = lax.optimization_barrier(mixed)
    selector = (jnp.arange(2) == part)[:, None, None]
    padded = jnp.where(selector, mixed.astype(jnp.float32), 0.0)
    return lax.psum_scatter(
        padded.astype(jnp.bfloat16), "fac", scatter_dimension=1, tiled=True
    ).astype(jnp.float32)


def solution(mesh):
    return jax.shard_map(
        local,
        mesh=mesh,
        in_specs=(P(None, "str", None), P(), P(), P(), P(), P(), P(), P(), P()),
        out_specs=P(None, "fac", "str"),
        check_vma=False,
    )
```

profile of v0, /device:TPU:0, one launch (start us, length us, event | category | flops | bytes accessed | tf_op | source)
XLA Modules:
  0.0 445.0 jit_solution(6631989853623679221)
XLA Ops:
  11.3 6.5 %copy.44 = bf16[1,512,4096]{1,2,0:T(8,128)(2,1)} copy(bf16[1,512,4096]{2,1,0:T(8,128)(2,1)} %constant_dynamic-slice_fusion.9) | data formatting | bytes 8388608
  21.9 6.4 %copy.28 = bf16[512,32,128]{2,0,1:T(8,128)(2,1)} copy(bf16[512,32,128]{0,2,1:T(8,128)(2,1)} %bitcast.181) | data formatting | bytes 8388608 | tf_op jit(solution)/shard_map/reshape | solution.py:13
  28.8 9.0 %gather_fusion.1 = bf16[96,512,128]{2,1,0:T(8,128)(2,1)} fusion(bf16[512,32,128]{2,0,1:T(8,128)(2,1)} %copy.28, s32[1024]{0:T(1024)S(1)} %pad_clamp_fusion.8), kind=kCustom, calls=%fused_computation.1 | custom fusion | bytes 25166208 | tf_op jit(solution)/shard_map/gather | solution.py:20
  37.8 9.0 %gather_fusion.3 = bf16[96,512,128]{2,1,0:T(8,128)(2,1)} fusion(bf16[512,32,128]{2,0,1:T(8,128)(2,1)} %copy.28, s32[1024]{0:T(1024)S(1)} %pad_clamp_fusion.6), kind=kCustom, calls=%fused_computation.3 | custom fusion | bytes 25166208 | tf_op jit(solution)/shard_map/gather | solution.py:20
  47.5 8.9 %fusion = bf16[1,512,8,128]{1,3,2,0:T(8,128)(2,1)S(1)} fusion(bf16[512,8,12,128]{3,0,2,1:T(8,128)(2,1)} %bitcast.174, bf16[12,128,128]{2,1,0:T(8,128)(2,1)S(1)} %gather_fusion.2), kind=kOutput, calls=%fused_computation.24 | convolution fusion | flops 1611137024 | bytes 14024704 | tf_op jit(solution)/shard_map/pajkc,krc->pajr/dot_general | solution.py:22
  60.8 9.0 %gather_fusion.4 = bf16[96,512,128]{2,1,0:T(8,128)(2,1)} fusion(bf16[512,32,128]{2,0,1:T(8,128)(2,1)} %copy.28, s32[1024]{0:T(1024)S(1)} %pad_clamp_fusion.5), kind=kCustom, calls=%fused_computation.4 | custom fusion | bytes 25166208 | tf_op jit(solution)/shard_map/gather | solution.py:20
  69.8 9.7 %fusion.2 = bf16[1,512,8,128]{1,3,2,0:T(8,128)(2,1)} fusion(bf16[512,8,12,128]{3,0,2,1:T(8,128)(2,1)} %bitcast.177, bf16[12,128,128]{2,1,0:T(8,128)(2,1)S(1)} %gather_fusion.2), kind=kOutput, calls=%fused_computation.26 | convolution fusion | flops 1611137024 | bytes 14024704 | tf_op jit(solution)/shard_map/pajkc,krc->pajr/dot_general | solution.py:22
  79.6 9.0 %gather_fusion.5 = bf16[96,512,128]{2,1,0:T(8,128)(2,1)} fusion(bf16[512,32,128]{2,0,1:T(8,128)(2,1)} %copy.28, s32[1024]{0:T(1024)S(1)} %pad_clamp_fusion.4), kind=kCustom, calls=%fused_computation.5 | custom fusion | bytes 25166208 | tf_op jit(solution)/shard_map/gather | solution.py:20
  88.6 8.8 %fusion.3 = bf16[1,512,8,128]{1,3,2,0:T(8,128)(2,1)S(1)} fusion(bf16[512,8,12,128]{3,0,2,1:T(8,128)(2,1)} %bitcast.176, bf16[12,128,128]{2,1,0:T(8,128)(2,1)S(1)} %gather_fusion.2), kind=kOutput, calls=%fused_computation.27 | convolution fusion | flops 1611137024 | bytes 14024704 | tf_op jit(solution)/shard_map/pajkc,krc->pajr/dot_general | solution.py:22
  98.0 36.5 %copy.56 = bf16[1,512,4096]{1,0,2:T(2,128)(2,1)} copy(bf16[1,512,4096]{1,2,0:T(8,128)(2,1)S(1)} %bitcast.178) | data formatting | bytes 8388608 | tf_op jit(solution)/shard_map/reshape | solution.py:26
  135.0 28.5 %reduce.4 = bf16[4096,512]{1,0:T(8,128)(2,1)} reduce(bf16[4096,1,512]{2,1,0:T(2,128)(2,1)} %bitcast.172, bf16[]{:T(256)} %broadcast.272), dimensions={1}, to_apply=%bitcast.167.reduce_sub_computation | reduce | bytes 8388610
  163.5 7.9 %reshape.535 = bf16[8,2,131072]{2,1,0:T(2,128)(2,1)} reshape(bf16[4096,512]{1,0:T(8,128)(2,1)} %reduce.4) | data formatting | bytes 8388608
  171.4 7.3 %all-to-all-start = ((bf16[8,2,131072]{2,1,0:T(2,128)(2,1)}), bf16[8,2,131072]{2,1,0:T(2,128)(2,1)}, u32[]{:S(2)}, u32[]{:S(2)}) async-start(bf16[8,2,131072]{2,1,0:T(2,128)(2,1)} %reshape.535), calls=%async_computation | async-start | bytes 8388608 | tf_op jit(solution)/shard_map/all_to_all | solution.py:74
  180.3 91.7 %all-to-all-done = bf16[8,2,131072]{2,1,0:T(2,128)(2,1)} async-done(((bf16[8,2,131072]{2,1,0:T(2,128)(2,1)}), bf16[8,2,131072]{2,1,0:T(2,128)(2,1)}, u32[]{:S(2)}, u32[]{:S(2)}) %all-to-all-start) | async-done | bytes 4194336 | tf_op jit(solution)/shard_map/all_to_all | solution.py:74
  272.0 8.8 %reshape.536 = bf16[4096,1,512]{2,1,0:T(2,128)(2,1)} reshape(bf16[8,2,131072]{2,1,0:T(2,128)(2,1)} %all-to-all-done) | data formatting | bytes 8388608
  280.8 6.6 %copy.43 = bf16[1,512,4096]{1,2,0:T(8,128)(2,1)} copy(bf16[1,512,4096]{1,0,2:T(2,128)(2,1)} %bitcast.173) | data formatting | bytes 8388608
  287.4 6.5 %copy.33 = bf16[1,8,512,512]{3,2,1,0:T(8,128)(2,1)} copy(bf16[1,8,512,512]{2,3,1,0:T(8,128)(2,1)} %bitcast.179) | data formatting | bytes 8388608 | tf_op jit(solution)/shard_map/all_to_all | solution.py:74
  297.8 9.0 %gather_fusion.6 = bf16[96,128,512]{2,1,0:T(8,128)(2,1)} fusion(bf16[32,128,512]{2,1,0:T(8,128)(2,1)} %multiply_bitcast_fusion, s32[1024]{0:T(1024)S(1)} %pad_clamp_fusion.3), kind=kCustom, calls=%fused_computation.6 | custom fusion | bytes 25166208 | tf_op jit(solution)/shard_map/gather | solution.py:42
  306.8 9.0 %gather_fusion.7 = bf16[96,128,512]{2,1,0:T(8,128)(2,1)} fusion(bf16[32,128,512]{2,1,0:T(8,128)(2,1)} %multiply_bitcast_fusion, s32[1024]{0:T(1024)S(1)} %pad_clamp_fusion.2), kind=kCustom, calls=%fused_computation.7 | custom fusion | bytes 25166208 | tf_op jit(solution)/shard_map/gather | solution.py:42
  315.8 5.9 %fusion.4 = bf16[1,8,128,512]{3,2,1,0:T(8,128)(2,1)S(1)} fusion(bf16[8,12,128,512]{3,2,1,0:T(8,128)(2,1)} %bitcast.168, bf16[12,128,128]{2,1,0:T(8,128)(2,1)S(1)} %gather_fusion), kind=kOutput, calls=%fused_computation.28 | convolution fusion | flops 1611137024 | bytes 14024704 | tf_op jit(solution)/shard_map/pjkcn,krc->pjrn/dot_general | solution.py:44
  327.0 9.0 %gather_fusion.8 = bf16[96,128,512]{2,1,0:T(8,128)(2,1)} fusion(bf16[32,128,512]{2,1,0:T(8,128)(2,1)} %multiply_bitcast_fusion, s32[1024]{0:T(1024)S(1)} %pad_clamp_fusion.1), kind=kCustom, calls=%fused_computation.8 | custom fusion | bytes 25166208 | tf_op jit(solution)/shard_map/gather | solution.py:42
  336.0 6.7 %fusion.6 = bf16[1,8,128,512]{3,2,1,0:T(8,128)(2,1)} fusion(bf16[8,12,128,512]{3,2,1,0:T(8,128)(2,1)} %bitcast.171, bf16[12,128,128]{2,1,0:T(8,128)(2,1)S(1)} %gather_fusion), kind=kOutput, calls=%fused_computation.30 | convolution fusion | flops 1611137024 | bytes 14024704 | tf_op jit(solution)/shard_map/pjkcn,krc->pjrn/dot_general | solution.py:44
  342.6 9.0 %gather_fusion.9 = bf16[96,128,512]{2,1,0:T(8,128)(2,1)} fusion(bf16[32,128,512]{2,1,0:T(8,128)(2,1)} %multiply_bitcast_fusion, s32[1024]{0:T(1024)S(1)} %pad_clamp_fusion), kind=kCustom, calls=%fused_computation.9 | custom fusion | bytes 25166208 | tf_op jit(solution)/shard_map/gather | solution.py:42
  363.3 70.7 %reduce-scatter.2.cloned.1.call-done = bf16[2,1024,512]{2,1,0:T(8,128)(2,1)} async-done(((bf16[2,4096,512]{2,1,0:T(8,128)(2,1)}), bf16[2,1024,512]{2,1,0:T(8,128)(2,1)}) %reduce-scatter.2.cloned.1.call-update) | async-done | bytes 2097168 | tf_op jit(solution)/shard_map/reduce_scatter | solution.py:83
  (78 shorter events, 42.0 us)
Async XLA Ops:
  6.5 40.3 %copy-start = (bf16[16,128,128]{2,1,0:T(8,128)(2,1)S(1)}, bf16[16,128,128]{2,1,0:T(8,128)(2,1)}, u32[]{:S(2)}) copy-start(bf16[16,128,128]{2,1,0:T(8,128)(2,1)} %param.16) | copy-start | bytes 1572868
  6.5 11.2 %copy-start.10 = (s32[2,4096]{1,0:T(2,128)S(1)}, s32[2,4096]{1,0:T(2,128)}, u32[]{:S(2)}) copy-start(s32[2,4096]{1,0:T(2,128)} %param.15) | copy-start | bytes 98308
  6.5 11.2 %copy-start.11 = (s32[2,4096]{1,0:T(2,128)S(1)}, s32[2,4096]{1,0:T(2,128)}, u32[]{:S(2)}) copy-start(s32[2,4096]{1,0:T(2,128)} %param.12) | copy-start | bytes 98308
  17.9 10.4 %copy-start.8 = (s32[2,32,12]{1,0,2:T(2,128)S(1)}, s32[2,32,12]{1,0,2:T(2,128)}, u32[]{:S(2)}) copy-start(s32[2,32,12]{1,0,2:T(2,128)} %param.10) | copy-start | bytes 9220
  17.9 10.8 %copy-start.12 = (s32[2,12]{1,0:T(2,128)S(1)}, s32[2,12]{1,0:T(2,128)}, u32[]{:S(2)}) copy-start(s32[2,12]{1,0:T(2,128)} %param.14) | copy-start | bytes 292
  17.9 10.8 %copy-start.13 = (s32[2,12]{1,0:T(2,128)S(1)}, s32[2,12]{1,0:T(2,128)}, u32[]{:S(2)}) copy-start(s32[2,12]{1,0:T(2,128)} %param.11) | copy-start | bytes 292
  47.4 8.9 %copy-start.3 = (bf16[96,512,128]{2,1,0:T(8,128)(2,1)S(1)}, bf16[96,512,128]{2,1,0:T(8,128)(2,1)}, u32[]{:S(2)}) copy-start(bf16[96,512,128]{2,1,0:T(8,128)(2,1)} %gather_fusion.3) | copy-start | bytes 37748740
  88.6 8.8 %copy-start.6 = (bf16[1,512,8,128]{1,3,2,0:T(8,128)(2,1)S(1)}, bf16[1,512,8,128]{1,3,2,0:T(8,128)(2,1)}, u32[]{:S(2)}) copy-start(bf16[1,512,8,128]{1,3,2,0:T(8,128)(2,1)} %fusion.2) | copy-start | bytes 3145732
  163.5 15.2 %copy-start.9 = (s32[2,32,12]{1,0,2:T(2,128)S(1)}, s32[2,32,12]{1,0,2:T(2,128)}, u32[]{:S(2)}) copy-start(s32[2,32,12]{1,0,2:T(2,128)} %param.13) | copy-start | bytes 9220
  163.5 16.0 %copy-start.7 = (bf16[16,128,128]{2,1,0:T(8,128)(2,1)S(1)}, bf16[16,128,128]{2,1,0:T(8,128)(2,1)}, u32[]{:S(2)}) copy-start(bf16[16,128,128]{2,1,0:T(8,128)(2,1)} %param.17) | copy-start | bytes 1572868
  171.4 100.6 %all-to-all-start = ((bf16[8,2,131072]{2,1,0:T(2,128)(2,1)}), bf16[8,2,131072]{2,1,0:T(2,128)(2,1)}, u32[]{:S(2)}, u32[]{:S(2)}) async-start(bf16[8,2,131072]{2,1,0:T(2,128)(2,1)} %reshape.535), calls=%async_computation | async-start | bytes 8388608 | tf_op jit(solution)/shard_map/all_to_all | solution.py:74
  178.7 255.2 %reduce-scatter.2.cloned.1.call-start = ((), (), s32[]{:S(2)}) async-start(), calls=%async_computation.2 | async-start | bytes 10485760 | tf_op jit(solution)/shard_map/reduce_scatter | solution.py:83
  315.8 8.2 %copy-start.2 = (bf16[96,128,512]{2,1,0:T(8,128)(2,1)S(1)}, bf16[96,128,512]{2,1,0:T(8,128)(2,1)}, u32[]{:S(2)}) copy-start(bf16[96,128,512]{2,1,0:T(8,128)(2,1)} %gather_fusion.7) | copy-start | bytes 37748740
  351.7 5.9 %copy-start.4 = (bf16[1,8,128,512]{3,2,1,0:T(8,128)(2,1)S(1)}, bf16[1,8,128,512]{3,2,1,0:T(8,128)(2,1)}, u32[]{:S(2)}) copy-start(bf16[1,8,128,512]{3,2,1,0:T(8,128)(2,1)} %fusion.5) | copy-start | bytes 3145732
  351.7 5.9 %copy-start.5 = (bf16[1,8,128,512]{3,2,1,0:T(8,128)(2,1)S(1)}, bf16[1,8,128,512]{3,2,1,0:T(8,128)(2,1)}, u32[]{:S(2)}) copy-start(bf16[1,8,128,512]{3,2,1,0:T(8,128)(2,1)} %fusion.6) | copy-start | bytes 3145732
  358.1 80.0 %copy-start.1 = (bf16[16,128,128]{2,1,0:T(8,128)(2,1)S(1)}, bf16[16,128,128]{2,1,0:T(8,128)(2,1)}, u32[]{:S(2)}) copy-start(bf16[16,128,128]{2,1,0:T(8,128)(2,1)} %param.16) | copy-start | bytes 1572868
Sparse Core Ops, SparseCore 0:
  363.4 70.5 reduce-scatter.1
where the time goes:
time: 446 us; the launch traced here: 445 us
  local copies, waits for them, and re-layouts  162 us (36%)
  waiting for transfers between devices  162 us (36%)
  matrix products  52.9 us (12%)
  other arithmetic  47.1 us (11%)
  between operations  13.7 us (3%)
  starting transfers between devices  7.33 us (2%)
    all_to_all x1, waiting for transfers between devices, local(): lax.all_to_all(half, 'str', split_axis=2, concat_axis=1, tiled=True)  91.7 us
    reduce_scatter x1, waiting for transfers between devices, local(): lax.psum_scatter(padded.astype(jnp.bfloat16), 'fac', scatter_dimension=1,...  70.7 us
    reshape x1, local copies, waits for them, and re-layouts, apply_beta(): jnp.concatenate(pieces, axis=2).reshape(part_count, height, column_count)  36.5 us
    gather x4, local copies, waits for them, and re-layouts, apply_beta(): gathered = blocks[:, :, chosen]  36.1 us
    gather x4, local copies, waits for them, and re-layouts, apply_alpha(): gathered = blocks[:, chosen]  36 us
    unnamed x41, local copies, waits for them, and re-layouts  33.3 us
    dot_general x4, matrix products, apply_beta(): jnp.einsum('pajkc,krc->pajr', gathered, weights, preferred_element_type=j...  31.5 us
    unnamed x1, other arithmetic  28.5 us
  transfers between devices with their start and end apart: 2, of which 2 were waited for; matrix products, arithmetic and copies ran while one was open for 0% of the time, Pallas kernels for 0%

commit v1 on v0

--- a/solution.py
+++ b/solution.py
@@ -2,6 +2,29 @@
 import jax.numpy as jnp
 from jax import lax
 from jax.sharding import PartitionSpec as P
+
+
+def split_up(array, dim, devices):
+    before, after = (array.shape[:dim], array.shape[dim + 1 :])
+    return jnp.moveaxis(array.reshape(*before, devices, -1, *after), dim, 0)
+
+
+def laid_out(parts, dim):
+    parts = jnp.moveaxis(parts, 0, dim)
+    dims = parts.shape
+    return parts.reshape(*dims[:dim], dims[dim] * dims[dim + 1], *dims[dim + 2 :])
+
+
+def exchange_directly(x, axis, split_dim, concat_dim):
+    size, here = (lax.axis_size(axis), lax.axis_index(axis))
+    blocks = split_up(x, split_dim, size)
+    whole = blocks
+    for step in range(1, size):
+        target, source = ((here + step) % size, (here - step) % size)
+        sent = lax.dynamic_index_in_dim(blocks, target, 0)
+        other = lax.ppermute(sent, axis, [(i, (i + step) % size) for i in range(size)])
+        whole = lax.dynamic_update_slice_in_dim(whole, other, source, axis=0)
+    return laid_out(whole, concat_dim)
 
 
 def apply_beta(amplitudes, block_ids, tile_ids, flips, tile_table):
@@ -71,11 +94,7 @@
     alpha_kinds = lax.dynamic_index_in_dim(alpha_tile, factor, 0, keepdims=False)
     alpha_signs = lax.dynamic_index_in_dim(alpha_flip, factor, 0, keepdims=False)
     mixed = apply_alpha(
-        lax.all_to_all(half, "str", split_axis=2, concat_axis=1, tiled=True),
-        alpha_ids,
-        alpha_kinds,
-        alpha_signs,
-        alpha_tiles,
+        exchange_directly(half, "str", 2, 1), alpha_ids, alpha_kinds, alpha_signs, alpha_tiles
     )
     mixed = lax.optimization_barrier(mixed)
     selector = (jnp.arange(2) == part)[:, None, None]

time: 446 us -> 361 us (0.81)
  local copies, waits for them, and re-layouts: 162 us -> 121 us
  waiting for transfers between devices: 162 us -> 132 us
  other arithmetic: 47.1 us -> 20.8 us
  starting transfers between devices: 7.33 us -> 18.5 us
    all_to_all x1 -> x0, waiting for transfers between devices: 91.7 us -> none  [local(): lax.all_to_all(half, 'str', split_axis=2, concat_axis=1, tiled=True)]
    reshape x1 -> x0, local copies, waits for them, and re-layouts: 36.5 us -> none  [apply_beta(): jnp.concatenate(pieces, axis=2).reshape(part_count, height, column_count)]
    ppermute x0 -> x7, waiting for transfers between devices: none -> 33 us  [exchange_directly(): lax.ppermute(sent, axis, [(i, (i + step) % size) for i in range(size)])]
    unnamed x1 -> x0, other arithmetic: 28.5 us -> none
    reduce_scatter x1, waiting for transfers between devices: 70.7 us -> 98.9 us  [local(): lax.psum_scatter(padded.astype(jnp.bfloat16), 'fac', scatter_dimension=1,...]
    unnamed x41 -> x35, local copies, waits for them, and re-layouts: 33.3 us -> 11.5 us
    ppermute x0 -> x7, starting transfers between devices: none -> 18.5 us  [exchange_directly(): lax.ppermute(sent, axis, [(i, (i + step) % size) for i in range(size)])]
    another operation x0 -> x9, local copies, waits for them, and re-layouts: none -> 11.8 us  [the longest x1 6.47 us: split_up(): return jnp.moveaxis(array.reshape(*before, devices, -1, *after), dim, 0)]
  transfers between devices with their start and end apart: 2 -> 8, of which waited for: 2 -> 3; matrix products, arithmetic and copies ran while one was open for 0% -> 6% of each run, Pallas kernels for 0% -> 0%
where the time goes in v1:
time: 361 us; the launch traced here: 360 us
  waiting for transfers between devices  132 us (37%)
  local copies, waits for them, and re-layouts  121 us (34%)
  matrix products  53.9 us (15%)
  other arithmetic  20.8 us (6%)
  starting transfers between devices  18.5 us (5%)
  between operations  13.7 us (4%)
    reduce_scatter x1, waiting for transfers between devices, local(): lax.psum_scatter(padded.astype(jnp.bfloat16), 'fac', scatter_dimension=1,...  98.9 us
    gather x4, local copies, waits for them, and re-layouts, apply_beta(): gathered = blocks[:, :, chosen]  36.1 us
    gather x4, local copies, waits for them, and re-layouts, apply_alpha(): gathered = blocks[:, chosen]  36.1 us
    ppermute x7, waiting for transfers between devices, exchange_directly(): lax.ppermute(sent, axis, [(i, (i + step) % size) for i in range(size)])  33 us
    dot_general x4, matrix products, apply_beta(): jnp.einsum('pajkc,krc->pajr', gathered, weights, preferred_element_type=j...  32.5 us
    dot_general x4, matrix products, apply_alpha(): jnp.einsum('pjkcn,krc->pjrn', gathered, weights, preferred_element_type=j...  21.4 us
    ppermute x7, starting transfers between devices, exchange_directly(): lax.ppermute(sent, axis, [(i, (i + step) % size) for i in range(size)])  18.5 us
    unnamed x35, local copies, waits for them, and re-layouts  11.5 us
  transfers between devices with their start and end apart: 8, of which 3 were waited for; matrix products, arithmetic and copies ran while one was open for 6% of the time, Pallas kernels for 0%

profile of v1, /device:TPU:0, one launch (start us, length us, event | category | flops | bytes accessed | tf_op | source)
XLA Modules:
  0.0 359.6 jit_solution(7498206489567525504)
XLA Ops:
  6.5 4.8 %constant_dynamic-slice_fusion.16 = bf16[1,512,4096]{2,1,0:T(8,128)(2,1)} fusion(bf16[2,512,4096]{2,1,0:T(8,128)(2,1)} %param.9, s32[]{:T(128)S(6)} %select_n.233), kind=kLoop, calls=%fused_computation.73 | loop fusion | bytes 8388612 | tf_op jit(solution)/shard_map/jit(dynamic_index_in_dim)/dynamic_slice | solution.py:88
  11.3 6.5 %copy.49 = bf16[1,512,4096]{1,2,0:T(8,128)(2,1)} copy(bf16[1,512,4096]{2,1,0:T(8,128)(2,1)} %constant_dynamic-slice_fusion.16) | data formatting | bytes 8388608
  21.8 6.5 %copy.28 = bf16[512,32,128]{2,0,1:T(8,128)(2,1)} copy(bf16[512,32,128]{0,2,1:T(8,128)(2,1)} %bitcast.181) | data formatting | bytes 8388608 | tf_op jit(solution)/shard_map/reshape | solution.py:36
  28.8 9.0 %gather_fusion.1 = bf16[96,512,128]{2,1,0:T(8,128)(2,1)} fusion(bf16[512,32,128]{2,0,1:T(8,128)(2,1)} %copy.28, s32[1024]{0:T(1024)S(1)} %pad_clamp_fusion.8), kind=kCustom, calls=%fused_computation.1 | custom fusion | bytes 25166208 | tf_op jit(solution)/shard_map/gather | solution.py:43
  37.8 9.0 %gather_fusion.3 = bf16[96,512,128]{2,1,0:T(8,128)(2,1)} fusion(bf16[512,32,128]{2,0,1:T(8,128)(2,1)} %copy.28, s32[1024]{0:T(1024)S(1)} %pad_clamp_fusion.6), kind=kCustom, calls=%fused_computation.3 | custom fusion | bytes 25166208 | tf_op jit(solution)/shard_map/gather | solution.py:43
  47.5 8.9 %fusion = bf16[1,512,8,128]{1,3,2,0:T(8,128)(2,1)S(1)} fusion(bf16[512,8,12,128]{3,0,2,1:T(8,128)(2,1)} %bitcast.175, bf16[12,128,128]{2,1,0:T(8,128)(2,1)S(1)} %gather_fusion.2), kind=kOutput, calls=%fused_computation.24 | convolution fusion | flops 1611137024 | bytes 14024704 | tf_op jit(solution)/shard_map/pajkc,krc->pajr/dot_general | solution.py:45
  56.4 4.2 %fusion.1 = bf16[1,512,8,128]{1,3,2,0:T(8,128)(2,1)S(1)} fusion(bf16[512,8,12,128]{3,0,2,1:T(8,128)(2,1)S(1)} %bitcast.176, bf16[12,128,128]{2,1,0:T(8,128)(2,1)S(1)} %gather_fusion.2), kind=kOutput, calls=%fused_computation.25 | convolution fusion | flops 1611137024 | bytes 14024704 | tf_op jit(solution)/shard_map/pajkc,krc->pajr/dot_general | solution.py:45
  60.8 9.0 %gather_fusion.4 = bf16[96,512,128]{2,1,0:T(8,128)(2,1)} fusion(bf16[512,32,128]{2,0,1:T(8,128)(2,1)} %copy.28, s32[1024]{0:T(1024)S(1)} %pad_clamp_fusion.5), kind=kCustom, calls=%fused_computation.4 | custom fusion | bytes 25166208 | tf_op jit(solution)/shard_map/gather | solution.py:43
  69.8 9.8 %fusion.2 = bf16[1,512,8,128]{1,3,2,0:T(8,128)(2,1)} fusion(bf16[512,8,12,128]{3,0,2,1:T(8,128)(2,1)} %bitcast.178, bf16[12,128,128]{2,1,0:T(8,128)(2,1)S(1)} %gather_fusion.2), kind=kOutput, calls=%fused_computation.26 | convolution fusion | flops 1611137024 | bytes 14024704 | tf_op jit(solution)/shard_map/pajkc,krc->pajr/dot_general | solution.py:45
  79.7 9.0 %gather_fusion.5 = bf16[96,512,128]{2,1,0:T(8,128)(2,1)} fusion(bf16[512,32,128]{2,0,1:T(8,128)(2,1)} %copy.28, s32[1024]{0:T(1024)S(1)} %pad_clamp_fusion.4), kind=kCustom, calls=%fused_computation.5 | custom fusion | bytes 25166208 | tf_op jit(solution)/shard_map/gather | solution.py:43
  88.7 9.7 %fusion.3 = bf16[1,512,8,128]{1,3,2,0:T(8,128)(2,1)} fusion(bf16[512,8,12,128]{3,0,2,1:T(8,128)(2,1)} %bitcast.177, bf16[12,128,128]{2,1,0:T(8,128)(2,1)S(1)} %gather_fusion.2), kind=kOutput, calls=%fused_computation.27 | convolution fusion | flops 1611137024 | bytes 14024704 | tf_op jit(solution)/shard_map/pajkc,krc->pajr/dot_general | solution.py:45
  120.1 6.5 %copy.32 = bf16[1,512,8,512]{3,1,2,0:T(8,128)(2,1)} copy(bf16[1,512,8,512]{1,3,2,0:T(8,128)(2,1)} %bitcast.174) | data formatting | bytes 8388608 | tf_op jit(solution)/shard_map/reshape;reshape | solution.py:9
  132.1 5.9 %collective-permute-start.6 = (bf16[1,1,512,512]{3,2,0,1:T(8,128)(2,1)S(1)}, bf16[1,1,512,512]{3,2,0,1:T(8,128)(2,1)S(1)}, u32[]{:S(2)}, u32[]{:S(2)}) collective-permute-start(bf16[1,1,512,512]{3,2,0,1:T(8,128)(2,1)S(1)} %bitcast.188), channel_id=1, source_target_pairs={{0,28},{4,0},{8,4},{12,8},{16,12},{20,16},{24,20},{28,24},{1,29},{... | collective-permute-start | bytes 1572872 | tf_op jit(solution)/shard_map/ppermute | solution.py:25
  139.9 29.9 %collective-permute-done.2 = bf16[1,1,512,512]{3,2,0,1:T(8,128)(2,1)} collective-permute-done((bf16[1,1,512,512]{3,2,0,1:T(8,128)(2,1)S(1)}, bf16[1,1,512,512]{3,2,0,1:T(8,128)(2,1)}, u32[]{:S(2)}, u32[]{:S(2)}) %collective-permute-start.2) | collective-permute-done | bytes 524320 | tf_op jit(solution)/shard_map/ppermute | solution.py:25
  184.1 9.0 %gather_fusion.6 = bf16[96,128,512]{2,1,0:T(8,128)(2,1)} fusion(bf16[32,128,512]{2,1,0:T(8,128)(2,1)} %multiply_bitcast_fusion, s32[1024]{0:T(1024)S(1)} %pad_clamp_fusion.3), kind=kCustom, calls=%fused_computation.6 | custom fusion | bytes 25166208 | tf_op jit(solution)/shard_map/gather | solution.py:65
  193.1 9.0 %gather_fusion.7 = bf16[96,128,512]{2,1,0:T(8,128)(2,1)} fusion(bf16[32,128,512]{2,1,0:T(8,128)(2,1)} %multiply_bitcast_fusion, s32[1024]{0:T(1024)S(1)} %pad_clamp_fusion.2), kind=kCustom, calls=%fused_computation.7 | custom fusion | bytes 25166208 | tf_op jit(solution)/shard_map/gather | solution.py:65
  202.1 5.9 %fusion.4 = bf16[1,8,128,512]{3,2,1,0:T(8,128)(2,1)S(1)} fusion(bf16[8,12,128,512]{3,2,1,0:T(8,128)(2,1)} %bitcast.169, bf16[12,128,128]{2,1,0:T(8,128)(2,1)S(1)} %gather_fusion), kind=kOutput, calls=%fused_computation.28 | convolution fusion | flops 1611137024 | bytes 14024704 | tf_op jit(solution)/shard_map/pjkcn,krc->pjrn/dot_general | solution.py:67
  213.3 9.0 %gather_fusion.8 = bf16[96,128,512]{2,1,0:T(8,128)(2,1)} fusion(bf16[32,128,512]{2,1,0:T(8,128)(2,1)} %multiply_bitcast_fusion, s32[1024]{0:T(1024)S(1)} %pad_clamp_fusion.1), kind=kCustom, calls=%fused_computation.8 | custom fusion | bytes 25166208 | tf_op jit(solution)/shard_map/gather | solution.py:65
  222.3 6.7 %fusion.6 = bf16[1,8,128,512]{3,2,1,0:T(8,128)(2,1)} fusion(bf16[8,12,128,512]{3,2,1,0:T(8,128)(2,1)} %bitcast.172, bf16[12,128,128]{2,1,0:T(8,128)(2,1)S(1)} %gather_fusion), kind=kOutput, calls=%fused_computation.30 | convolution fusion | flops 1611137024 | bytes 14024704 | tf_op jit(solution)/shard_map/pjkcn,krc->pjrn/dot_general | solution.py:67
  229.0 9.0 %gather_fusion.9 = bf16[96,128,512]{2,1,0:T(8,128)(2,1)} fusion(bf16[32,128,512]{2,1,0:T(8,128)(2,1)} %multiply_bitcast_fusion, s32[1024]{0:T(1024)S(1)} %pad_clamp_fusion), kind=kCustom, calls=%fused_computation.9 | custom fusion | bytes 25166208 | tf_op jit(solution)/shard_map/gather | solution.py:65
  238.0 5.9 %fusion.7 = bf16[1,8,128,512]{3,2,1,0:T(8,128)(2,1)S(1)} fusion(bf16[8,12,128,512]{3,2,1,0:T(8,128)(2,1)} %bitcast.171, bf16[12,128,128]{2,1,0:T(8,128)(2,1)S(1)} %gather_fusion), kind=kOutput, calls=%fused_computation.31 | convolution fusion | flops 1611137024 | bytes 14024704 | tf_op jit(solution)/shard_map/pjkcn,krc->pjrn/dot_general | solution.py:67
  244.5 5.1 %select_convert_fusion = bf16[2,4096,512]{2,1,0:T(8,128)(2,1)} fusion(bf16[4096,512]{1,0:T(8,128)(2,1)S(1)} %bitcast.182, pred[2]{0:T(512)(128)(4,1)S(1)} %iota_compare_fusion), kind=kLoop, calls=%fused_computation.10 | loop fusion | flops 4194304 | bytes 12582914 | tf_op jit(solution)/shard_map/convert_element_type | solution.py:103
  249.7 98.9 %reduce-scatter.2.cloned.1.call-done = bf16[2,1024,512]{2,1,0:T(8,128)(2,1)} async-done(((bf16[2,4096,512]{2,1,0:T(8,128)(2,1)}), bf16[2,1024,512]{2,1,0:T(8,128)(2,1)}) %reduce-scatter.2.cloned.1.call-update) | async-done | bytes 2097168 | tf_op jit(solution)/shard_map/reduce_scatter | solution.py:102
  348.5 4.2 %convert_element_type.112 = f32[2,1024,512]{2,1,0:T(8,128)} convert(bf16[2,1024,512]{2,1,0:T(8,128)(2,1)} %reduce-scatter.2.cloned.1.call-done) | non-fusion elementwise | flops 1048576 | bytes 6291456 | tf_op jit(solution)/shard_map/convert_element_type | solution.py:104
  (98 shorter events, 54.6 us)
Async XLA Ops:
  6.5 40.3 %copy-start = (bf16[16,128,128]{2,1,0:T(8,128)(2,1)S(1)}, bf16[16,128,128]{2,1,0:T(8,128)(2,1)}, u32[]{:S(2)}) copy-start(bf16[16,128,128]{2,1,0:T(8,128)(2,1)} %param.16) | copy-start | bytes 1572868
  6.5 342.0 %reduce-scatter.2.cloned.1.call-start = ((), (), s32[]{:S(2)}) async-start(), calls=%async_computation.1 | async-start | bytes 10485760 | tf_op jit(solution)/shard_map/reduce_scatter | solution.py:102
  11.3 6.5 %copy-start.9 = (s32[2,4096]{1,0:T(2,128)S(1)}, s32[2,4096]{1,0:T(2,128)}, u32[]{:S(2)}) copy-start(s32[2,4096]{1,0:T(2,128)} %param.12) | copy-start | bytes 98308
  21.8 6.5 %copy-start.7 = (s32[2,32,12]{1,0,2:T(2,128)S(1)}, s32[2,32,12]{1,0,2:T(2,128)}, u32[]{:S(2)}) copy-start(s32[2,32,12]{1,0,2:T(2,128)} %param.10) | copy-start | bytes 9220
  21.8 6.8 %copy-start.11 = (s32[2,12]{1,0:T(2,128)S(1)}, s32[2,12]{1,0:T(2,128)}, u32[]{:S(2)}) copy-start(s32[2,12]{1,0:T(2,128)} %param.14) | copy-start | bytes 292
  21.8 6.9 %copy-start.12 = (s32[2,12]{1,0:T(2,128)S(1)}, s32[2,12]{1,0:T(2,128)}, u32[]{:S(2)}) copy-start(s32[2,12]{1,0:T(2,128)} %param.11) | copy-start | bytes 292
  47.5 8.9 %copy-start.4 = (bf16[96,512,128]{2,1,0:T(8,128)(2,1)S(1)}, bf16[96,512,128]{2,1,0:T(8,128)(2,1)}, u32[]{:S(2)}) copy-start(bf16[96,512,128]{2,1,0:T(8,128)(2,1)} %gather_fusion.3) | copy-start | bytes 37748740
  101.2 2.0 copy-start.3
  104.4 14.9 %copy-start.8 = (s32[2,32,12]{1,0,2:T(2,128)S(1)}, s32[2,32,12]{1,0,2:T(2,128)}, u32[]{:S(2)}) copy-start(s32[2,32,12]{1,0,2:T(2,128)} %param.13) | copy-start | bytes 9220
  106.5 22.3 %collective-permute-start = (bf16[1,1,512,512]{3,2,0,1:T(8,128)(2,1)}, bf16[1,1,512,512]{3,2,0,1:T(8,128)(2,1)}, u32[]{:S(2)}, u32[]{:S(2)}) collective-permute-start(bf16[1,1,512,512]{3,2,0,1:T(8,128)(2,1)} %bitcast.187), channel_id=1, source_target_pairs={{0,4},{4,8},{8,12},{12,16},{16,20},{20,24},{24,28},{28,0},{1,5},{5... | collective-permute-start | bytes 1572872 | tf_op jit(solution)/shard_map/ppermute | solution.py:25
  110.4 21.7 %collective-permute-start.1 = (bf16[1,1,512,512]{3,2,0,1:T(8,128)(2,1)}, bf16[1,1,512,512]{3,2,0,1:T(8,128)(2,1)}, u32[]{:S(2)}, u32[]{:S(2)}) collective-permute-start(bf16[1,1,512,512]{3,2,0,1:T(8,128)(2,1)} %bitcast.186), channel_id=1, source_target_pairs={{0,8},{4,12},{8,16},{12,20},{16,24},{20,28},{24,0},{28,4},{1,9},{5... | collective-permute-start | bytes 1572872 | tf_op jit(solution)/shard_map/ppermute | solution.py:25
  112.2 57.5 %collective-permute-start.2 = (bf16[1,1,512,512]{3,2,0,1:T(8,128)(2,1)S(1)}, bf16[1,1,512,512]{3,2,0,1:T(8,128)(2,1)}, u32[]{:S(2)}, u32[]{:S(2)}) collective-permute-start(bf16[1,1,512,512]{3,2,0,1:T(8,128)(2,1)S(1)} %bitcast.185), channel_id=1, source_target_pairs={{0,12},{4,16},{8,20},{12,24},{16,28},{20,0},{24,4},{28,8},{1,13},{... | collective-permute-start | bytes 1572872 | tf_op jit(solution)/shard_map/ppermute | solution.py:25
  115.0 56.6 %collective-permute-start.3 = (bf16[1,1,512,512]{3,2,0,1:T(8,128)(2,1)S(1)}, bf16[1,1,512,512]{3,2,0,1:T(8,128)(2,1)}, u32[]{:S(2)}, u32[]{:S(2)}) collective-permute-start(bf16[1,1,512,512]{3,2,0,1:T(8,128)(2,1)S(1)} %bitcast.184), channel_id=1, source_target_pairs={{0,16},{4,20},{8,24},{12,28},{16,0},{20,4},{24,8},{28,12},{1,17},{... | collective-permute-start | bytes 1572872 | tf_op jit(solution)/shard_map/ppermute | solution.py:25
  116.6 56.9 %collective-permute-start.4 = (bf16[1,1,512,512]{3,2,0,1:T(8,128)(2,1)S(1)}, bf16[1,1,512,512]{3,2,0,1:T(8,128)(2,1)}, u32[]{:S(2)}, u32[]{:S(2)}) collective-permute-start(bf16[1,1,512,512]{3,2,0,1:T(8,128)(2,1)S(1)} %bitcast.183), channel_id=1, source_target_pairs={{0,20},{4,24},{8,28},{12,0},{16,4},{20,8},{24,12},{28,16},{1,21},{... | collective-permute-start | bytes 1572872 | tf_op jit(solution)/shard_map/ppermute | solution.py:25
  120.1 8.6 %copy-start.10 = (s32[2,4096]{1,0:T(2,128)S(1)}, s32[2,4096]{1,0:T(2,128)}, u32[]{:S(2)}) copy-start(s32[2,4096]{1,0:T(2,128)} %param.15) | copy-start | bytes 98308
  128.8 46.6 %collective-permute-start.5 = (bf16[1,1,512,512]{3,2,0,1:T(8,128)(2,1)S(1)}, bf16[1,1,512,512]{3,2,0,1:T(8,128)(2,1)S(1)}, u32[]{:S(2)}, u32[]{:S(2)}) collective-permute-start(bf16[1,1,512,512]{3,2,0,1:T(8,128)(2,1)S(1)} %bitcast.189), channel_id=1, source_target_pairs={{0,24},{4,28},{8,0},{12,4},{16,8},{20,12},{24,16},{28,20},{1,25},{... | collective-permute-start | bytes 1572872 | tf_op jit(solution)/shard_map/ppermute | solution.py:25
  132.1 47.2 %collective-permute-start.6 = (bf16[1,1,512,512]{3,2,0,1:T(8,128)(2,1)S(1)}, bf16[1,1,512,512]{3,2,0,1:T(8,128)(2,1)S(1)}, u32[]{:S(2)}, u32[]{:S(2)}) collective-permute-start(bf16[1,1,512,512]{3,2,0,1:T(8,128)(2,1)S(1)} %bitcast.188), channel_id=1, source_target_pairs={{0,28},{4,0},{8,4},{12,8},{16,12},{20,16},{24,20},{28,24},{1,29},{... | collective-permute-start | bytes 1572872 | tf_op jit(solution)/shard_map/ppermute | solution.py:25
  202.1 8.2 %copy-start.2 = (bf16[96,128,512]{2,1,0:T(8,128)(2,1)S(1)}, bf16[96,128,512]{2,1,0:T(8,128)(2,1)}, u32[]{:S(2)}) copy-start(bf16[96,128,512]{2,1,0:T(8,128)(2,1)} %gather_fusion.7) | copy-start | bytes 37748740
  238.0 5.9 %copy-start.5 = (bf16[1,8,128,512]{3,2,1,0:T(8,128)(2,1)S(1)}, bf16[1,8,128,512]{3,2,1,0:T(8,128)(2,1)}, u32[]{:S(2)}) copy-start(bf16[1,8,128,512]{3,2,1,0:T(8,128)(2,1)} %fusion.5) | copy-start | bytes 3145732
  238.0 5.9 %copy-start.6 = (bf16[1,8,128,512]{3,2,1,0:T(8,128)(2,1)S(1)}, bf16[1,8,128,512]{3,2,1,0:T(8,128)(2,1)}, u32[]{:S(2)}) copy-start(bf16[1,8,128,512]{3,2,1,0:T(8,128)(2,1)} %fusion.6) | copy-start | bytes 3145732
  249.6 103.1 %copy-start.1 = (bf16[16,128,128]{2,1,0:T(8,128)(2,1)S(1)}, bf16[16,128,128]{2,1,0:T(8,128)(2,1)}, u32[]{:S(2)}) copy-start(bf16[16,128,128]{2,1,0:T(8,128)(2,1)} %param.16) | copy-start | bytes 1572868
Sparse Core Ops, SparseCore 0:
  249.8 98.7 reduce-scatter.1
